TPU v7x, 512 devices: a whole 4x4x16 slice. The times are simulated.
512 devices in a mesh: row: 32 (over x, z_lo), col: 16 (over y, z_hi, core).
Axes of the slice: x: 4, y: 4, z: 16 (z_hi: 2, z_lo: 8; z = z_hi * 8 + z_lo), core: 2. Of those that a mesh axis runs over, the one named last changes fastest.
Arguments:
- traces: bfloat16 [32, 2048, 2048], P(None, 'row', 'col'), may hold values from -6 to 6
- source_pos: int32 [2048], P('row'), may hold values from 0 to 16383
- receiver_pos: int32 [2048], replicated, may hold values from 0 to 16383
- aperture_list: int32 [128, 1024], P('row'), may hold values from 0 to 2047, as said below
- band_index: int32 [16384], P('row'), may hold values from 0 to 31
- weight_tiles: bfloat16 [32, 2, 128], replicated, may hold values from -4 to 4
Outputs:
- primaries: bfloat16 [32, 2048, 2048], P(None, 'row', 'col')
- image: float32 [2048, 16384], P('col', 'row')
Inputs may be any that keep to these rules, and one draw needn't show every extreme that they name: `aperture_list`: the 1024 receivers listed for one tile are distinct.
All inputs are finite; a program needn't handle non-finite values.
Results may differ from a plain program's by a relative error of at most 0.012.
Values may be sent and summed in bfloat16 or wider, within the bound.
A program may use at most 64 MiB of HBM per device.

v0:
```python
import math
import jax
import jax.numpy as jnp
from jax import lax
from jax.sharding import PartitionSpec as P

NFFT = 4096
NF = 4


def phase_tables(samples):
    freq_bins = (2 * jnp.arange(NF, dtype=jnp.int32) + 1) * (NFFT // (4 * NF))
    sample_ticks = jnp.arange(samples, dtype=jnp.int32)
    phase_turns = freq_bins[:, None] * sample_ticks[None, :] % NFFT
    phase_angle = phase_turns.astype(jnp.float32) * (2.0 * math.pi / NFFT)
    return (jnp.cos(phase_angle), jnp.sin(phase_angle))


def aperture_matrix(tile_index_lists, positions, columns, first_row, row_count, spread_len):
    tile_count, listed = tile_index_lists.shape
    col_width = columns.shape[0]
    inside = (tile_index_lists >= first_row) & (tile_index_lists < first_row + row_count)
    local_index = jnp.where(inside, tile_index_lists - first_row, row_count)
    tile_rows = jnp.broadcast_to(
        jnp.arange(tile_count, dtype=jnp.int32)[:, None], tile_index_lists.shape
    )
    member = (
        jnp.zeros((tile_count, row_count), jnp.float32)
        .at[tile_rows, local_index]
        .add(1.0, mode="drop")
    )
    widened = jnp.repeat(member.T, col_width // tile_count, axis=1)
    offset = (positions[:, None] - columns[None, :]).astype(jnp.float32) / spread_len
    taper_weight = 1.0 / (1.0 + offset * offset)
    return (widened * taper_weight * (2.0 / math.sqrt(listed))).astype(jnp.bfloat16)


def shot_weights(positions, columns, spread_len):
    offset = (positions[:, None] - columns[None, :]).astype(jnp.float32) / spread_len
    return 1.0 / (1.0 + offset * offset)


def complex_product(left_section, right_section):
    real_real = jnp.einsum(
        "qju,quy->qjy", left_section[0], right_section[0], preferred_element_type=jnp.float32
    )
    imag_imag = jnp.einsum(
        "qju,quy->qjy", left_section[1], right_section[1], preferred_element_type=jnp.float32
    )
    real_imag = jnp.einsum(
        "qju,quy->qjy", left_section[0], right_section[1], preferred_element_type=jnp.float32
    )
    imag_real = jnp.einsum(
        "qju,quy->qjy", left_section[1], right_section[0], preferred_element_type=jnp.float32
    )
    return jnp.stack([real_real - imag_imag, real_imag + imag_real])


def slab_stack(slab_block, aperture, stacking_weights):
    depth_slab_samples, shot_count, listed_rows = slab_block.shape
    stacked = jnp.dot(
        slab_block.reshape(depth_slab_samples * shot_count, listed_rows),
        aperture,
        preferred_element_type=jnp.float32,
    )
    stacked = stacked.reshape(depth_slab_samples, shot_count, aperture.shape[1])
    return jnp.sum(stacked * stacking_weights[None], axis=1)


def per_device(traces, source_pos, receiver_pos, aperture_list, band_index, weight_tiles):
    samples, shot_count, recv_count = traces.shape
    col_count = lax.axis_size("col")
    surface_count = recv_count * col_count
    image_panel_width = band_index.shape[0]
    depth_slab_samples = samples // col_count
    cosine, sine_table = phase_tables(samples)
    forward = (jnp.concatenate([cosine, -sine_table], 0) / math.sqrt(samples)).astype(jnp.bfloat16)
    spectra = jnp.dot(
        forward,
        traces.reshape(samples, shot_count * recv_count),
        preferred_element_type=jnp.float32,
    )
    spectra = spectra.astype(jnp.bfloat16).reshape(2, NF, shot_count, recv_count)
    columns_whole = lax.all_gather(spectra, "row", axis=2, tiled=True)
    summed = complex_product(lax.all_gather(spectra, "col", axis=3, tiled=True), columns_whole)
    multiples = -summed / math.sqrt(surface_count)
    inverse = jnp.concatenate([cosine, -sine_table], 0).T / math.sqrt(NF)
    wave_field = jnp.dot(
        inverse,
        multiples.reshape(2 * NF, shot_count * recv_count),
        precision=lax.Precision.HIGHEST,
        preferred_element_type=jnp.float32,
    )
    primaries = (
        traces.astype(jnp.float32) - wave_field.reshape(samples, shot_count, recv_count)
    ).astype(jnp.bfloat16)
    columns = lax.axis_index("row") * image_panel_width + jnp.arange(
        image_panel_width, dtype=jnp.int32
    )
    spread_len = image_panel_width * lax.axis_size("row") // 4
    stacking_weights = shot_weights(source_pos, columns, spread_len)
    slab_block = lax.all_to_all(primaries, "col", split_axis=0, concat_axis=2, tiled=True)
    aperture = aperture_matrix(aperture_list, receiver_pos, columns, 0, surface_count, spread_len)
    stacked = slab_stack(slab_block, aperture, stacking_weights)
    column_stack = (stacked / math.sqrt(shot_count)).astype(jnp.bfloat16)
    tile_kinds = weight_tiles.shape[0]
    select = band_index[None, :] == jnp.arange(tile_kinds, dtype=jnp.int32)[:, None]
    widened = jnp.where(select[:, None, :], column_stack[None], jnp.zeros((), jnp.bfloat16))
    image_out = jnp.einsum(
        "kz,kx->zx",
        weight_tiles.reshape(tile_kinds * depth_slab_samples, weight_tiles.shape[2]),
        widened.reshape(tile_kinds * depth_slab_samples, image_panel_width),
        preferred_element_type=jnp.float32,
    )
    return (primaries, image_out)


def solution(mesh):
    placed = (P(None, "row", "col"), P("row"), P(), P("row", None), P("row"), P())
    return jax.shard_map(
        per_device,
        mesh=mesh,
        in_specs=placed,
        out_specs=(P(None, "row", "col"), P("col", "row")),
        check_vma=False,
    )
```

profile of v0, /device:TPU:1, one launch (start us, length us, event | category | flops | bytes accessed | tf_op | source)
XLA Modules:
  0.0 404.6 jit_solution(7858936798405555199)
XLA Ops:
  7.2 0.0 copy-start
  7.2 0.0 all-gather.3.cloned.1.call-start
  7.2 0.1 fusion.30
  7.4 1.4 fusion.10
  8.8 0.7 copy.33
  9.5 0.0 all-gather.3.cloned.1.call-update
  9.5 0.0 all-gather.5.cloned.1.call-start
  9.5 0.7 all-gather.5.cloned.1.call-update
  10.3 0.7 fusion.19
  11.0 0.7 multiply_reduce_fusion
  11.7 0.8 and_reduce_fusion
  12.5 95.1 %all-gather.3.cloned.1.call-done = bf16[2,4,64,2048]{3,2,1,0:T(8,128)(2,1)} async-done(((bf16[2,4,64,128]{3,2,1,0:T(8,128)(2,1)}), bf16[2,4,64,2048]{3,2,1,0:T(8,128)(2,1)}) %all-gather.3.cloned.1.call-update) | async-done | bytes 2097168 | tf_op jit(solution)/shard_map/all_gather | solution.py:85
  107.6 211.9 %all-gather.5.cloned.1.call-done = bf16[2,4,2048,128]{3,2,1,0:T(8,128)(2,1)} async-done(((bf16[2,4,64,128]{3,2,1,0:T(8,128)(2,1)}), bf16[2,4,2048,128]{3,2,1,0:T(8,128)(2,1)}) %all-gather.5.cloned.1.call-update) | async-done | bytes 4194320 | tf_op jit(solution)/shard_map/all_gather | solution.py:84
  319.5 2.5 fusion.1
  322.0 2.4 fusion
  324.5 0.0 copy-start.1
  324.5 0.5 fusion.7
  325.0 0.5 fusion.9
  325.5 1.3 fusion.4
  326.8 1.0 copy.30
  327.8 33.6 %all-to-all-start = ((bf16[32,64,128]{2,1,0:T(8,128)(2,1)}), bf16[32,64,128]{2,1,0:T(8,128)(2,1)S(1)}, u32[]{:S(2)}, u32[]{:S(2)}) async-start(bf16[32,64,128]{2,1,0:T(8,128)(2,1)} %copy.30), calls=%async_computation | async-start | bytes 1048576 | tf_op jit(solution)/shard_map/all_to_all | solution.py:102
  361.5 22.1 %scatter_custom_fusion = f32[8192]{0:T(1024)S(1)} fusion(s32[4096]{0:T(1024)S(1)} %bitcast.76, f32[4096]{0:T(1024)S(1)} %broadcast.205, f32[]{:T(128)} %constant.56.clone.1), kind=kCustom, calls=%fused_computation.41 | custom fusion | flops 4096 | bytes 32772
  383.7 0.0 copy-start.3
  383.7 0.4 copy.28
  384.1 8.6 %multiply_convert_fusion = bf16[2048,4,128]{2,1,0:T(4,128)(2,1)} fusion(s32[4,128]{1,0:T(4,128)S(1)} %add_add_fusion, s32[2048]{0:T(1024)S(1)} %copy-done.2, f32[2048,4]{1,0:T(8,128)S(1)} %copy.28), kind=kLoop, calls=%fused_computation.2 | loop fusion | flops 9437184 | bytes 2140160 | tf_op jit(solution)/shard_map/convert_element_type | solution.py:35
  392.6 2.7 reshape.161
  395.5 0.1 add_divide_fusion
  395.6 0.3 copy.49
  395.9 0.2 dot_general.40
  396.2 0.5 fusion.5
  396.7 0.2 convolution_bitcast_fusion
  396.9 0.8 copy.31
  (23 shorter events, 0.1 us)
Async XLA Ops:
  7.2 389.5 %copy-start = (bf16[32,2,128]{2,1,0:T(2,128)(2,1)S(1)}, bf16[32,2,128]{2,1,0:T(2,128)(2,1)}, u32[]{:S(2)}) copy-start(bf16[32,2,128]{2,1,0:T(2,128)(2,1)} %param.11) | copy-start | bytes 49156
  7.2 100.4 %all-gather.3.cloned.1.call-start = ((), (), s32[]{:S(2)}) async-start(), calls=%async_computation.1 | async-start | bytes 2228224 | tf_op jit(solution)/shard_map/all_gather | solution.py:85
  9.5 310.0 %all-gather.5.cloned.1.call-start = ((), (), s32[]{:S(2)}) async-start(), calls=%async_computation.2 | async-start | bytes 4325376 | tf_op jit(solution)/shard_map/all_gather | solution.py:84
  107.6 216.9 %copy-start.6 = (bf16[2,4,64,2048]{3,2,1,0:T(8,128)(2,1)S(1)}, bf16[2,4,64,2048]{3,2,1,0:T(8,128)(2,1)}, u32[]{:S(2)}) copy-start(bf16[2,4,64,2048]{3,2,1,0:T(8,128)(2,1)} %all-gather.3.cloned.1.call-done) | copy-start | bytes 6291460
  319.5 5.0 %copy-start.5 = (bf16[2,4,2048,128]{3,2,1,0:T(8,128)(2,1)S(1)}, bf16[2,4,2048,128]{3,2,1,0:T(8,128)(2,1)}, u32[]{:S(2)}) copy-start(bf16[2,4,2048,128]{3,2,1,0:T(8,128)(2,1)} %all-gather.5.cloned.1.call-done) | copy-start | bytes 12582916
  324.5 1.1 copy-start.1
  325.0 59.1 %copy-start.2 = (s32[2048]{0:T(1024)S(1)}, s32[2048]{0:T(1024)}, u32[]{:S(2)}) copy-start(s32[2048]{0:T(1024)} %param.8) | copy-start | bytes 24580
  327.8 67.7 %all-to-all-start = ((bf16[32,64,128]{2,1,0:T(8,128)(2,1)}), bf16[32,64,128]{2,1,0:T(8,128)(2,1)S(1)}, u32[]{:S(2)}, u32[]{:S(2)}) async-start(bf16[32,64,128]{2,1,0:T(8,128)(2,1)} %copy.30), calls=%async_computation | async-start | bytes 1048576 | tf_op jit(solution)/shard_map/all_to_all | solution.py:102
  383.7 11.8 %copy-start.3 = (s32[512]{0:T(512)S(1)}, s32[512]{0:T(512)}, u32[]{:S(2)}) copy-start(s32[512]{0:T(512)} %param.10) | copy-start | bytes 6148
  383.7 11.8 %copy-start.4 = (s32[64]{0:T(128)S(1)}, s32[64]{0:T(128)}, u32[]{:S(2)}) copy-start(s32[64]{0:T(128)} %param.7) | copy-start | bytes 772
Sparse Core Ops, SparseCore 0:
  11.7 95.8 all-gather.2
  110.2 209.1 all-gather.4
where the time goes:
time: 405 us
  waiting for transfers between devices  308 us (76%)
  starting transfers between devices  33.7 us (8%)
  other arithmetic  33.2 us (8%)
  between operations  14.3 us (4%)
  matrix products  9.38 us (2%)
  local copies, waits for them, and re-layouts  6.27 us (2%)
    all_gather x1, waiting for transfers between devices, per_device(): columns_whole = lax.all_gather(spectra, 'row', axis=2, tiled=True)  212 us
    all_gather x1, waiting for transfers between devices, per_device(): lax.all_gather(spectra, 'col', axis=3, tiled=True)  95.1 us
    all_to_all x1, starting transfers between devices, per_device(): lax.all_to_all(primaries, 'col', split_axis=0, concat_axis=2, tiled=True)  33.6 us
    unnamed x4, other arithmetic  23.6 us
    convert_element_type x1, other arithmetic, aperture_matrix(): (widened * taper_weight * (2.0 / math.sqrt(listed))).astype(jnp.bfloat16)  8.57 us
  transfers between devices with their start and end apart: 3, of which 2 were waited for; matrix products, arithmetic and copies ran while one was open for 9% of the time, Pallas kernels for 0%

commit v1 on v0

--- a/solution.py
+++ b/solution.py
@@ -6,6 +6,11 @@
 
 NFFT = 4096
 NF = 4
+
+
+def all_by_exchange(x, mesh_axis, d):
+    outgoing = jnp.stack([x] * lax.axis_size(mesh_axis))
+    return jnp.concatenate(lax.all_to_all(outgoing, mesh_axis, 0, 0), axis=d)
 
 
 def phase_tables(samples):
@@ -81,7 +86,7 @@
         preferred_element_type=jnp.float32,
     )
     spectra = spectra.astype(jnp.bfloat16).reshape(2, NF, shot_count, recv_count)
-    columns_whole = lax.all_gather(spectra, "row", axis=2, tiled=True)
+    columns_whole = all_by_exchange(spectra, "row", 2)
     summed = complex_product(lax.all_gather(spectra, "col", axis=3, tiled=True), columns_whole)
     multiples = -summed / math.sqrt(surface_count)
     inverse = jnp.concatenate([cosine, -sine_table], 0).T / math.sqrt(NF)

time: 405 us -> 309 us (0.76)
  the two profiles are of different devices: /device:TPU:1 before, /device:TPU:43 now
where the time goes in v1:
time: 309 us; the launch traced here: 308 us
  waiting for transfers between devices  213 us (69%)
  other arithmetic  31.1 us (10%)
  starting transfers between devices  27 us (9%)
  between operations  14.3 us (5%)
  local copies, waits for them, and re-layouts  14.1 us (5%)
  matrix products  8.1 us (3%)
    all_to_all x1, waiting for transfers between devices, all_by_exchange(): return jnp.concatenate(lax.all_to_all(outgoing, mesh_axis, 0, 0), axis=d)  213 us
    unnamed x4, other arithmetic  22.2 us
    all_to_all x1, starting transfers between devices, all_by_exchange(): return jnp.concatenate(lax.all_to_all(outgoing, mesh_axis, 0, 0), axis=d)  14.9 us
    all_to_all x1, starting transfers between devices, per_device(): lax.all_to_all(primaries, 'col', split_axis=0, concat_axis=2, tiled=True)  12.1 us
    convert_element_type x1, other arithmetic, aperture_matrix(): (widened * taper_weight * (2.0 / math.sqrt(listed))).astype(jnp.bfloat16)  8.55 us
  transfers between devices with their start and end apart: 3, of which 1 were waited for; matrix products, arithmetic and copies ran while one was open for 13% of the time, Pallas kernels for 0%

profile of v1, /device:TPU:43, one launch (start us, length us, event | category | flops | bytes accessed | tf_op | source)
XLA Modules:
  0.0 308.1 jit_solution(104268075594324993)
XLA Ops:
  7.2 0.1 fusion.26
  7.3 1.4 fusion.2
  8.8 3.0 stack.12
  11.8 14.9 %all-to-all-start = ((bf16[32,2,4,64,128]{4,3,2,1,0:T(8,128)(2,1)}), bf16[32,2,4,64,128]{4,3,2,1,0:T(8,128)(2,1)}, u32[]{:S(2)}, u32[]{:S(2)}) async-start(bf16[32,2,4,64,128]{4,3,2,1,0:T(8,128)(2,1)} %stack.12), calls=%async_computation | async-start | bytes 8388608 | tf_op jit(solution)/shard_map/all_to_all | solution.py:13
  26.7 0.0 all-gather.2.cloned.1.call-start
  26.8 0.7 all-gather.2.cloned.1.call-update
  27.5 0.1 multiply_reduce_fusion
  27.6 0.1 and_reduce_fusion
  27.7 212.8 %all-to-all-done = bf16[32,2,4,64,128]{4,3,2,1,0:T(8,128)(2,1)} async-done(((bf16[32,2,4,64,128]{4,3,2,1,0:T(8,128)(2,1)}), bf16[32,2,4,64,128]{4,3,2,1,0:T(8,128)(2,1)}, u32[]{:S(2)}, u32[]{:S(2)}) %all-to-all-start) | async-done | bytes 4194336 | tf_op jit(solution)/shard_map/all_to_all | solution.py:13
  240.5 3.2 %fusion.32 = (bf16[1,4,32,64,128]{4,3,1,0,2:T(8,128)(2,1)S(1)}, bf16[1,4,32,64,128]{4,3,1,0,2:T(8,128)(2,1)S(1)}) fusion(bf16[2,4,32,64,128]{4,3,1,0,2:T(8,128)(2,1)} %bitcast.2), kind=kLoop, calls=%fused_computation.63 | loop fusion | bytes 8388608 | tf_op jit(solution)/shard_map/slice | solution.py:50
  243.7 0.2 copy.29
  243.9 1.5 copy.28
  245.4 1.9 fusion.5
  247.3 0.0 copy-done.1
  247.3 1.9 fusion.6
  249.2 0.0 copy-done.2
  249.2 0.5 fusion.3
  249.8 0.5 fusion.4
  250.3 0.5 copy-done.3
  250.8 1.2 fusion
  252.0 1.0 copy.34
  253.0 12.1 %all-to-all-start.1 = ((bf16[32,64,128]{2,1,0:T(8,128)(2,1)}), bf16[32,64,128]{2,1,0:T(8,128)(2,1)S(1)}, u32[]{:S(2)}, u32[]{:S(2)}) async-start(bf16[32,64,128]{2,1,0:T(8,128)(2,1)} %copy.34), calls=%async_computation.1 | async-start | bytes 1048576 | tf_op jit(solution)/shard_map/all_to_all | solution.py:107
  265.1 22.1 %scatter_custom_fusion = f32[8192]{0:T(1024)S(1)} fusion(s32[4096]{0:T(1024)S(1)} %bitcast.71, f32[4096]{0:T(1024)S(1)} %broadcast.206, f32[]{:T(128)} %constant.56.clone.1), kind=kCustom, calls=%fused_computation.37 | custom fusion | flops 4096 | bytes 32772
  287.2 0.4 copy.32
  287.6 8.5 %multiply_convert_fusion = bf16[2048,4,128]{2,1,0:T(4,128)(2,1)} fusion(s32[4,128]{1,0:T(4,128)S(1)} %add_add_fusion, s32[2048]{0:T(1024)S(1)} %copy-done.6, f32[2048,4]{1,0:T(8,128)S(1)} %copy.32), kind=kLoop, calls=%fused_computation.2 | loop fusion | flops 9437184 | bytes 2140160 | tf_op jit(solution)/shard_map/convert_element_type | solution.py:40
  296.2 2.8 reshape.172
  299.0 0.1 add_divide_fusion
  299.1 0.3 copy.53
  299.5 0.2 dot_general.40
  299.7 0.5 fusion.1
  300.2 0.2 convolution_bitcast_fusion
  300.4 0.8 copy.35
  (34 shorter events, 0.2 us)
Async XLA Ops:
  7.2 293.0 %copy-start = (bf16[32,2,128]{2,1,0:T(2,128)(2,1)S(1)}, bf16[32,2,128]{2,1,0:T(2,128)(2,1)}, u32[]{:S(2)}) copy-start(bf16[32,2,128]{2,1,0:T(2,128)(2,1)} %param.11) | copy-start | bytes 49156
  8.8 3.1 copy-start.4
  11.8 15.6 %copy-start.5 = (s32[4,1024]{1,0:T(4,128)S(1)}, s32[4,1024]{1,0:T(4,128)}, u32[]{:S(2)}) copy-start(s32[4,1024]{1,0:T(4,128)} %param.9) | copy-start | bytes 49156
  11.8 15.7 %copy-start.9 = (s32[2]{0:T(128)S(1)}, s32[2]{0:T(128)}, u32[]{:S(2)}) copy-start(s32[2]{0:T(128)} %constant.68) | copy-start | bytes 28
  11.8 15.8 %copy-start.10 = (s32[2]{0:T(128)S(1)}, s32[2]{0:T(128)}, u32[]{:S(2)}) copy-start(s32[2]{0:T(128)} %constant.71) | copy-start | bytes 28
  11.8 228.6 %all-to-all-start = ((bf16[32,2,4,64,128]{4,3,2,1,0:T(8,128)(2,1)}), bf16[32,2,4,64,128]{4,3,2,1,0:T(8,128)(2,1)}, u32[]{:S(2)}, u32[]{:S(2)}) async-start(bf16[32,2,4,64,128]{4,3,2,1,0:T(8,128)(2,1)} %stack.12), calls=%async_computation | async-start | bytes 8388608 | tf_op jit(solution)/shard_map/all_to_all | solution.py:13
  26.7 218.7 %all-gather.2.cloned.1.call-start = ((), (), s32[]{:S(2)}) async-start(), calls=%async_computation.2 | async-start | bytes 2228224 | tf_op jit(solution)/shard_map/all_gather | solution.py:90
  245.4 1.9 copy-start.1
  247.3 1.9 copy-start.2
  249.7 1.0 copy-start.3
  250.8 36.8 %copy-start.6 = (s32[2048]{0:T(1024)S(1)}, s32[2048]{0:T(1024)}, u32[]{:S(2)}) copy-start(s32[2048]{0:T(1024)} %param.8) | copy-start | bytes 24580
  253.0 46.1 %all-to-all-start.1 = ((bf16[32,64,128]{2,1,0:T(8,128)(2,1)}), bf16[32,64,128]{2,1,0:T(8,128)(2,1)S(1)}, u32[]{:S(2)}, u32[]{:S(2)}) async-start(bf16[32,64,128]{2,1,0:T(8,128)(2,1)} %copy.34), calls=%async_computation.1 | async-start | bytes 1048576 | tf_op jit(solution)/shard_map/all_to_all | solution.py:107
  296.2 2.8 copy-start.7
  296.2 2.8 copy-start.8
Sparse Core Ops, SparseCore 0:
  31.3 97.0 all-gather.1
